TPU v7x, 128 devices: a whole 4x4x4 slice. The times are simulated.
128 devices in a mesh: ma: 32 (over z, x, core), band: 4 (over y).
Axes of the slice: x: 4, y: 4, z: 4, core: 2. Of those that a mesh axis runs over, the one named last changes fastest.
Arguments:
- observed: bfloat16 [1024, 64, 1024], P(('ma', 'band')), may hold values from -6 to 6
- eigenvalues: float32 [1024, 1024], P(('ma', 'band')), may hold values from 0.05 to 20
- kl_basis: bfloat16 [1024, 1024, 512], P(('ma', 'band')), may hold values from -0.1875 to 0.1875
- band_deriv: bfloat16 [40, 512, 512], P('band'), may hold values from -0.15625 to 0.15625, as said below
- counts: int32 [1024], P(('ma', 'band')), may hold values from 128 to 1024, as said below
Outputs:
- mode_power: float32 [1024, 40], P('ma', 'band')
- band_power: float32 [40], P('band')
Inputs may be any that keep to these rules, and one draw needn't show every extreme that they name: counts[m] is the number of leading KL modes of m-mode m that are kept; some m-mode keeps 1024 and some keeps 1024 // 8. Each band_deriv[a] is symmetric.
All inputs are finite; a program needn't handle non-finite values.
Results may differ from a plain program's by a relative error of at most 0.0018.
Values may be sent and summed in bfloat16 or wider, within the bound.
A program may use at most 64 MiB of HBM per device.

v0:
```python
import jax
import jax.numpy as jnp
from jax import lax
from jax.sharding import Mesh
from jax.sharding import PartitionSpec as P

MA_BAND = ("ma_0", "ma_1", "ma_2", "band")
MA = ("ma_0", "ma_1", "ma_2")


def from_everyone(x, axis):
    count = lax.axis_size(axis)
    return lax.all_to_all(jnp.broadcast_to(x[None], (count, *x.shape)), axis, 0, 0, tiled=True)


def laid_out(tiles, dim):
    tiles = jnp.moveaxis(tiles, 0, dim)
    shape = tiles.shape
    return tiles.reshape(*shape[:dim], shape[dim] * shape[dim + 1], *shape[dim + 2 :])


def gather_directly(x, axis, dim):
    tiles = from_everyone(x, axis)
    return laid_out(tiles, dim)


def over_axes(x, axes):
    for axis in axes:
        x = lax.psum(x, axis)
    return x


def weigh(observed, eigenvalues, counts):
    position = lax.broadcasted_iota(jnp.int32, eigenvalues.shape, 1)
    inside = position < counts[:, None]
    weights = jnp.where(inside, 1.0 / (1.0 + eigenvalues), jnp.zeros_like(eigenvalues))
    return (observed.astype(jnp.float32) * weights[:, None, :]).astype(jnp.bfloat16)


def project_padded(weighted, kl_basis):
    return jnp.einsum("msi,miw->msw", weighted, kl_basis, preferred_element_type=jnp.float32)


def band_quadratic(vectors, matrices):
    mode_count = vectors.shape[0]
    flattened = vectors.reshape(mode_count * vectors.shape[1], vectors.shape[2])

    def one_band(matrix):
        mapped = jnp.dot(flattened, matrix, preferred_element_type=jnp.float32)
        return jnp.sum((mapped * flattened).reshape(mode_count, -1), axis=1)

    return lax.map(one_band, matrices)


def per_device(observed, eigenvalues, kl_basis, band_deriv, counts):
    samples = observed.shape[1]
    own_bands = band_deriv.shape[0]
    weighted = weigh(observed, eigenvalues, counts)
    projected = project_padded(weighted, kl_basis)
    projected = projected.astype(jnp.bfloat16)
    quadratic = band_quadratic(gather_directly(projected, "band", 0), band_deriv)
    mode_power = jnp.transpose(quadratic) / samples
    partial_sum = jnp.sum(mode_power, axis=0)
    band_start = lax.axis_index("band") * own_bands
    scattered = jnp.zeros((own_bands * lax.axis_size("band"),), jnp.float32)
    scattered = lax.dynamic_update_slice_in_dim(scattered, partial_sum, band_start, 0)
    every_band, live_total = (
        over_axes(scattered, MA_BAND),
        over_axes(jnp.sum(counts).astype(jnp.float32), MA_BAND),
    )
    band_total = lax.dynamic_slice_in_dim(every_band, band_start, own_bands, 0)
    band_power = observed.shape[2] * band_total / live_total
    return (mode_power, band_power)


def solution(mesh):
    split = Mesh(
        mesh.devices.reshape(4, 4, 2, mesh.shape["band"]), ("ma_0", "ma_1", "ma_2", "band")
    )
    return jax.shard_map(
        per_device,
        mesh=split,
        in_specs=(
            P(MA_BAND, None, None),
            P(MA_BAND, None),
            P(MA_BAND, None, None),
            P("band", None, None),
            P(MA_BAND),
        ),
        out_specs=(P(MA, "band"), P("band")),
        check_vma=False,
    )
```

profile of v0, /device:TPU:0, one launch (start us, length us, event | category | flops | bytes accessed | tf_op | source)
XLA Modules:
  0.0 119.2 jit_solution(1673569421186196398)
XLA Ops:
  0.6 0.8 divide_select_fusion
  1.5 5.2 %convolution_convert_fusion = bf16[8,64,512]{2,1,0:T(8,128)(2,1)S(1)} fusion(bf16[8,1024,512]{2,1,0:T(8,128)(2,1)} %param.9, bf16[8,64,1024]{2,1,0:T(8,128)(2,1)} %param.7, f32[8,1024]{1,0:T(8,128)S(1)} %divide_select_fusion), kind=kOutput, calls=%fused_computation.6 | convolution fusion | flops 538705920 | bytes 9994240 | tf_op jit(solution)/shard_map/msi,miw->msw/dot_general | solution.py:41
  6.7 1.6 %broadcast_in_dim.23 = bf16[4,8,64,512]{3,2,1,0:T(8,128)(2,1)} broadcast(bf16[8,64,512]{2,1,0:T(8,128)(2,1)S(1)} %convolution_convert_fusion), dimensions={1,2,3} | broadcast | bytes 2621440 | tf_op jit(solution)/shard_map/broadcast_in_dim | solution.py:13
  8.3 4.6 %all-to-all-start = ((bf16[4,8,64,512]{3,2,1,0:T(8,128)(2,1)}), bf16[4,8,64,512]{3,2,1,0:T(8,128)(2,1)S(1)}, u32[]{:S(2)}, u32[]{:S(2)}) async-start(bf16[4,8,64,512]{3,2,1,0:T(8,128)(2,1)} %broadcast_in_dim.23), calls=%async_computation | async-start | bytes 4194304 | tf_op jit(solution)/shard_map/all_to_all | solution.py:13
  12.9 0.6 reduce_sum.35
  14.1 25.0 %all-to-all-done = bf16[4,8,64,512]{3,2,1,0:T(8,128)(2,1)S(1)} async-done(((bf16[4,8,64,512]{3,2,1,0:T(8,128)(2,1)}), bf16[4,8,64,512]{3,2,1,0:T(8,128)(2,1)S(1)}, u32[]{:S(2)}, u32[]{:S(2)}) %all-to-all-start) | async-done | bytes 2097184 | tf_op jit(solution)/shard_map/all_to_all | solution.py:13
  39.2 2.5 %copy.9 = bf16[2048,512]{0,1:T(8,128)(2,1)} copy(bf16[2048,512]{1,0:T(8,128)(2,1)S(1)} %bitcast.21) | data formatting | bytes 4194304 | tf_op jit(solution)/shard_map/while | solution.py:52
  41.7 39.3 %while.10 = (s32[]{:T(128)}, f32[10,32]{1,0:T(8,128)S(1)}, bf16[10,512,512]{2,1,0:T(8,128)(2,1)}, bf16[2048,512]{0,1:T(8,128)(2,1)}, s32[]{:T(128)}, /*index=5*/f32[]{:T(128)}, s32[]{:T(128)}) while((s32[]{:T(128)}, f32[10,32]{1,0:T(8,128)S(1)}, bf16[10,512,512]{2,1,0:T(8,128)(2,1)}, bf16[2048,512]{0,1:T(8,128)(2,1)}, s32[]{:T(128)}, ...), condition=%wide.region_3.4_spmd, body=%wide.region_0.3_spmd.sunk | while | flops 1076887552 | bytes 4752341 | solution.py:52
  41.7 3.7 %fusion.12 = f32[2048]{0:T(1024)S(1)} fusion(bf16[2048,512]{0,1:T(8,128)(2,1)} %get-tuple-element.93, bf16[10,512,512]{2,1,0:T(8,128)(2,1)} %get-tuple-element.92, s32[]{:T(128)} %get-tuple-element.83), kind=kOutput, calls=%fused_computation.1.clone.1 | convolution fusion | flops 1076885504 | bytes 4727296 | tf_op jit(solution)/shard_map/while/body/eval_jaxpr/dot_general | solution.py:49
  45.4 0.1 reduce_sum.43
  45.6 3.7 %fusion.12 = f32[2048]{0:T(1024)S(1)} fusion(bf16[2048,512]{0,1:T(8,128)(2,1)} %get-tuple-element.93, bf16[10,512,512]{2,1,0:T(8,128)(2,1)} %get-tuple-element.92, s32[]{:T(128)} %get-tuple-element.83), kind=kOutput, calls=%fused_computation.1.clone.1 | convolution fusion | flops 1076885504 | bytes 4727296 | tf_op jit(solution)/shard_map/while/body/eval_jaxpr/dot_general | solution.py:49
  49.4 0.1 reduce_sum.43
  49.5 3.7 %fusion.12 = f32[2048]{0:T(1024)S(1)} fusion(bf16[2048,512]{0,1:T(8,128)(2,1)} %get-tuple-element.93, bf16[10,512,512]{2,1,0:T(8,128)(2,1)} %get-tuple-element.92, s32[]{:T(128)} %get-tuple-element.83), kind=kOutput, calls=%fused_computation.1.clone.1 | convolution fusion | flops 1076885504 | bytes 4727296 | tf_op jit(solution)/shard_map/while/body/eval_jaxpr/dot_general | solution.py:49
  53.3 0.1 reduce_sum.43
  53.4 3.7 %fusion.12 = f32[2048]{0:T(1024)S(1)} fusion(bf16[2048,512]{0,1:T(8,128)(2,1)} %get-tuple-element.93, bf16[10,512,512]{2,1,0:T(8,128)(2,1)} %get-tuple-element.92, s32[]{:T(128)} %get-tuple-element.83), kind=kOutput, calls=%fused_computation.1.clone.1 | convolution fusion | flops 1076885504 | bytes 4727296 | tf_op jit(solution)/shard_map/while/body/eval_jaxpr/dot_general | solution.py:49
  57.4 3.7 %fusion.12 = f32[2048]{0:T(1024)S(1)} fusion(bf16[2048,512]{0,1:T(8,128)(2,1)} %get-tuple-element.93, bf16[10,512,512]{2,1,0:T(8,128)(2,1)} %get-tuple-element.92, s32[]{:T(128)} %get-tuple-element.83), kind=kOutput, calls=%fused_computation.1.clone.1 | convolution fusion | flops 1076885504 | bytes 4727296 | tf_op jit(solution)/shard_map/while/body/eval_jaxpr/dot_general | solution.py:49
  61.3 3.7 %fusion.12 = f32[2048]{0:T(1024)S(1)} fusion(bf16[2048,512]{0,1:T(8,128)(2,1)} %get-tuple-element.93, bf16[10,512,512]{2,1,0:T(8,128)(2,1)} %get-tuple-element.92, s32[]{:T(128)} %get-tuple-element.83), kind=kOutput, calls=%fused_computation.1.clone.1 | convolution fusion | flops 1076885504 | bytes 4727296 | tf_op jit(solution)/shard_map/while/body/eval_jaxpr/dot_general | solution.py:49
  65.2 3.7 %fusion.12 = f32[2048]{0:T(1024)S(1)} fusion(bf16[2048,512]{0,1:T(8,128)(2,1)} %get-tuple-element.93, bf16[10,512,512]{2,1,0:T(8,128)(2,1)} %get-tuple-element.92, s32[]{:T(128)} %get-tuple-element.83), kind=kOutput, calls=%fused_computation.1.clone.1 | convolution fusion | flops 1076885504 | bytes 4727296 | tf_op jit(solution)/shard_map/while/body/eval_jaxpr/dot_general | solution.py:49
  69.0 0.1 reduce_sum.43
  69.2 3.7 %fusion.12 = f32[2048]{0:T(1024)S(1)} fusion(bf16[2048,512]{0,1:T(8,128)(2,1)} %get-tuple-element.93, bf16[10,512,512]{2,1,0:T(8,128)(2,1)} %get-tuple-element.92, s32[]{:T(128)} %get-tuple-element.83), kind=kOutput, calls=%fused_computation.1.clone.1 | convolution fusion | flops 1076885504 | bytes 4727296 | tf_op jit(solution)/shard_map/while/body/eval_jaxpr/dot_general | solution.py:49
  72.9 0.1 reduce_sum.43
  73.1 3.7 %fusion.12 = f32[2048]{0:T(1024)S(1)} fusion(bf16[2048,512]{0,1:T(8,128)(2,1)} %get-tuple-element.93, bf16[10,512,512]{2,1,0:T(8,128)(2,1)} %get-tuple-element.92, s32[]{:T(128)} %get-tuple-element.83), kind=kOutput, calls=%fused_computation.1.clone.1 | convolution fusion | flops 1076885504 | bytes 4727296 | tf_op jit(solution)/shard_map/while/body/eval_jaxpr/dot_general | solution.py:49
  76.9 0.1 reduce_sum.43
  77.0 3.7 %fusion.12 = f32[2048]{0:T(1024)S(1)} fusion(bf16[2048,512]{0,1:T(8,128)(2,1)} %get-tuple-element.93, bf16[10,512,512]{2,1,0:T(8,128)(2,1)} %get-tuple-element.92, s32[]{:T(128)} %get-tuple-element.83), kind=kOutput, calls=%fused_computation.1.clone.1 | convolution fusion | flops 1076885504 | bytes 4727296 | tf_op jit(solution)/shard_map/while/body/eval_jaxpr/dot_general | solution.py:49
  80.8 0.1 reduce_sum.43
  81.0 0.7 multiply_reduce_fusion
  81.7 0.2 dynamic_update_slice.7
  81.9 12.3 %all-reduce.2 = (f32[40]{0:T(128)S(1)}, f32[]{:T(128)}) all-reduce(f32[40]{0:T(128)S(1)} %dynamic_update_slice.7, f32[]{:T(128)S(6)} %convert_element_type.18), channel_id=1, replica_groups=mesh['ma_0'=4,'ma_1'=4,'ma_2'=2,'band'=4] {'ma_0'}, use_global_device_ids=true, to_apply=%region_5.6 | all-reduce | flops 41 | bytes 328 | tf_op jit(solution)/shard_map/psum | solution.py:29
  94.2 11.1 %all-reduce.1 = (f32[40]{0:T(128)S(1)}, f32[]{:T(128)}) all-reduce(f32[40]{0:T(128)S(1)} %get-tuple-element.45, f32[]{:T(128)} %get-tuple-element.46), channel_id=1, replica_groups=mesh['ma_0'=4,'ma_1'=4,'ma_2'=2,'band'=4] {'ma_1'}, use_global_device_ids=true, to_apply=%region_6.7 | all-reduce | flops 41 | bytes 328 | tf_op jit(solution)/shard_map/psum | solution.py:29
  105.3 3.1 %all-reduce.3 = (f32[40]{0:T(128)S(1)}, f32[]{:T(128)}) all-reduce(f32[40]{0:T(128)S(1)} %get-tuple-element.43, f32[]{:T(128)} %get-tuple-element.44), channel_id=1, replica_groups=mesh['ma_0'=4,'ma_1'=4,'ma_2'=2,'band'=4] {'ma_2'}, use_global_device_ids=true, to_apply=%region_7.8 | all-reduce | flops 41 | bytes 328 | tf_op jit(solution)/shard_map/psum | solution.py:29
  108.3 9.6 %all-reduce = (f32[40]{0:T(128)S(1)}, f32[]{:T(128)}) all-reduce(f32[40]{0:T(128)S(1)} %get-tuple-element.47, f32[]{:T(128)} %get-tuple-element.48), channel_id=1, replica_groups=mesh['ma_0'=4,'ma_1'=4,'ma_2'=2,'band'=4] {'band'}, use_global_device_ids=true, to_apply=%region_8.9 | all-reduce | flops 41 | bytes 328 | tf_op jit(solution)/shard_map/psum | solution.py:29
  117.9 1.3 %multiply_divide_fusion = f32[10]{0:T(128)} fusion(f32[40]{0:T(128)S(1)} %get-tuple-element.41, s32[]{:T(128)S(6)} %select_n.9, f32[]{:T(128)} %get-tuple-element.42), kind=kLoop, calls=%fused_computation.12 | loop fusion | flops 20 | bytes 88 | tf_op jit(solution)/shard_map/div | solution.py:72
  (27 shorter events, 1.4 us)
Async XLA Ops:
  6.7 6.2 %copy-start = (s32[8]{0:T(128)S(1)}, s32[8]{0:T(128)}, u32[]{:S(2)}) copy-start(s32[8]{0:T(128)} %param.11) | copy-start | bytes 100
  8.3 30.9 %all-to-all-start = ((bf16[4,8,64,512]{3,2,1,0:T(8,128)(2,1)}), bf16[4,8,64,512]{3,2,1,0:T(8,128)(2,1)S(1)}, u32[]{:S(2)}, u32[]{:S(2)}) async-start(bf16[4,8,64,512]{3,2,1,0:T(8,128)(2,1)} %broadcast_in_dim.23), calls=%async_computation | async-start | bytes 4194304 | tf_op jit(solution)/shard_map/all_to_all | solution.py:13
where the time goes:
time: 120 us; the launch traced here: 119 us
  matrix products  42.1 us (35%)
  blocking collectives  36 us (30%)
  waiting for transfers between devices  25 us (21%)
  local copies, waits for them, and re-layouts  5.36 us (4%)
  other arithmetic  4.61 us (4%)
  starting transfers between devices  4.57 us (4%)
  between operations  1.31 us (1%)
    dot_general x10, matrix products, one_band(): mapped = jnp.dot(flattened, matrix, preferred_element_type=jnp.float32)  36.9 us
    psum x4, blocking collectives, over_axes(): x = lax.psum(x, axis)  36 us
    all_to_all x1, waiting for transfers between devices, from_everyone(): lax.all_to_all(jnp.broadcast_to(x[None], (count, *x.shape)), axis, 0, 0,...  25 us
    dot_general x1, matrix products, project_padded(): jnp.einsum('msi,miw->msw', weighted, kl_basis, preferred_element_type=jnp...  5.21 us
    all_to_all x1, starting transfers between devices, from_everyone(): lax.all_to_all(jnp.broadcast_to(x[None], (count, *x.shape)), axis, 0, 0,...  4.57 us
    while x1, local copies, waits for them, and re-layouts, band_quadratic(): return lax.map(one_band, matrices)  2.47 us
  transfers between devices with their start and end apart: 1, of which 1 were waited for; matrix products, arithmetic and copies ran while one was open for 1% of the time, Pallas kernels for 0%

commit v1 on v0

--- a/solution.py
+++ b/solution.py
@@ -26,7 +26,7 @@
 
 def over_axes(x, axes):
     for axis in axes:
-        x = lax.psum(x, axis)
+        x = jnp.sum(lax.all_gather(x, axis), axis=0)
     return x
 
 

time: 120 us -> 122 us (1.017)
  waiting for transfers between devices: 25 us -> 6.25 us
  blocking collectives: 36 us -> 44.6 us
  local copies, waits for them, and re-layouts: 5.36 us -> 13.5 us
  other arithmetic: 4.61 us -> 7.19 us
  between operations: 1.31 us -> 3.27 us
    psum x4 -> x0, blocking collectives: 36 us -> none  [over_axes(): x = lax.psum(x, axis)]
    unnamed x0 -> x4, blocking collectives: none -> 33.6 us
    all_to_all x1, waiting for transfers between devices: 25 us -> 6.25 us  [from_everyone(): lax.all_to_all(jnp.broadcast_to(x[None], (count, *x.shape)), axis, 0, 0,...]
    all_gather x0 -> x1, blocking collectives: none -> 11 us  [over_axes(): x = jnp.sum(lax.all_gather(x, axis), axis=0)]
    unnamed x2 -> x29, local copies, waits for them, and re-layouts: 0.01 us -> 7.92 us
    reduce_sum x0 -> x8, other arithmetic: none -> 2.58 us  [over_axes(): x = jnp.sum(lax.all_gather(x, axis), axis=0)]
  transfers between devices with their start and end apart: 1 -> 1, of which waited for: 1 -> 1; matrix products, arithmetic and copies ran while one was open for 1% -> 5% of each run, Pallas kernels for 0% -> 0%
where the time goes in v1:
time: 122 us
  blocking collectives  44.6 us (37%)
  matrix products  42.1 us (35%)
  local copies, waits for them, and re-layouts  13.5 us (11%)
  other arithmetic  7.19 us (6%)
  waiting for transfers between devices  6.25 us (5%)
  starting transfers between devices  4.57 us (4%)
  between operations  3.27 us (3%)
    dot_general x10, matrix products, one_band(): mapped = jnp.dot(flattened, matrix, preferred_element_type=jnp.float32)  36.9 us
    unnamed x4, blocking collectives  33.6 us
    all_gather x1, blocking collectives, over_axes(): x = jnp.sum(lax.all_gather(x, axis), axis=0)  11 us
    unnamed x29, local copies, waits for them, and re-layouts  7.92 us
    all_to_all x1, waiting for transfers between devices, from_everyone(): lax.all_to_all(jnp.broadcast_to(x[None], (count, *x.shape)), axis, 0, 0,...  6.25 us
    dot_general x1, matrix products, project_padded(): jnp.einsum('msi,miw->msw', weighted, kl_basis, preferred_element_type=jnp...  5.22 us
    all_to_all x1, starting transfers between devices, from_everyone(): lax.all_to_all(jnp.broadcast_to(x[None], (count, *x.shape)), axis, 0, 0,...  4.57 us
    reduce_sum x8, other arithmetic, over_axes(): x = jnp.sum(lax.all_gather(x, axis), axis=0)  2.58 us
  transfers between devices with their start and end apart: 1, of which 1 were waited for; matrix products, arithmetic and copies ran while one was open for 5% of the time, Pallas kernels for 0%

profile of v1, /device:TPU:0, one launch (start us, length us, event | category | flops | bytes accessed | tf_op | source)
XLA Modules:
  0.0 121.6 jit_solution(12237323592387387142)
XLA Ops:
  0.6 0.8 divide_select_fusion
  1.5 5.2 %convolution_convert_fusion = bf16[8,64,512]{2,1,0:T(8,128)(2,1)S(1)} fusion(bf16[8,1024,512]{2,1,0:T(8,128)(2,1)} %param.9, bf16[8,64,1024]{2,1,0:T(8,128)(2,1)} %param.7, f32[8,1024]{1,0:T(8,128)S(1)} %divide_select_fusion), kind=kOutput, calls=%fused_computation.6 | convolution fusion | flops 538705920 | bytes 9994240 | tf_op jit(solution)/shard_map/msi,miw->msw/dot_general | solution.py:41
  6.7 1.6 %broadcast_in_dim.23 = bf16[4,8,64,512]{3,2,1,0:T(8,128)(2,1)} broadcast(bf16[8,64,512]{2,1,0:T(8,128)(2,1)S(1)} %convolution_convert_fusion), dimensions={1,2,3} | broadcast | bytes 2621440 | tf_op jit(solution)/shard_map/broadcast_in_dim | solution.py:13
  8.4 4.6 %all-to-all-start = ((bf16[4,8,64,512]{3,2,1,0:T(8,128)(2,1)}), bf16[4,8,64,512]{3,2,1,0:T(8,128)(2,1)S(1)}, u32[]{:S(2)}, u32[]{:S(2)}) async-start(bf16[4,8,64,512]{3,2,1,0:T(8,128)(2,1)} %broadcast_in_dim.23), calls=%async_computation | async-start | bytes 4194304 | tf_op jit(solution)/shard_map/all_to_all | solution.py:13
  12.9 0.6 reduce_sum.111
  14.8 0.8 dynamic-update-slice.3
  15.6 11.7 %all-reduce.3 = f32[4]{0:T(128)S(1)} all-reduce(f32[4]{0:T(128)S(1)} %dynamic-update-slice.3), channel_id=1, replica_groups=mesh['ma_0'=4,'ma_1'=4,'ma_2'=2,'band'=4] {'ma_0'}, use_global_device_ids=true, to_apply=%add.3 | all-reduce | flops 4 | bytes 32
  29.8 0.6 dynamic-slice.2
  31.0 0.6 reduce_sum.112
  31.6 1.4 %dynamic-update-slice.4 = f32[4]{0:T(128)S(1)} dynamic-update-slice(f32[4]{0:T(128)S(1)} %broadcast.21.clone, f32[1]{0:T(128)} %bitcast.11, u32[]{:T(128)} %bitcast.12) | dynamic-update-slice | bytes 12
  33.0 6.3 %all-to-all-done = bf16[4,8,64,512]{3,2,1,0:T(8,128)(2,1)S(1)} async-done(((bf16[4,8,64,512]{3,2,1,0:T(8,128)(2,1)}), bf16[4,8,64,512]{3,2,1,0:T(8,128)(2,1)S(1)}, u32[]{:S(2)}, u32[]{:S(2)}) %all-to-all-start) | async-done | bytes 2097184 | tf_op jit(solution)/shard_map/all_to_all | solution.py:13
  39.3 2.5 %copy.10 = bf16[2048,512]{0,1:T(8,128)(2,1)} copy(bf16[2048,512]{1,0:T(8,128)(2,1)S(1)} %bitcast.33) | data formatting | bytes 4194304 | tf_op jit(solution)/shard_map/while | solution.py:52
  41.7 39.3 %while.10 = (s32[]{:T(128)}, f32[10,32]{1,0:T(8,128)S(1)}, bf16[10,512,512]{2,1,0:T(8,128)(2,1)}, bf16[2048,512]{0,1:T(8,128)(2,1)}, s32[]{:T(128)}, /*index=5*/f32[]{:T(128)}, s32[]{:T(128)}) while((s32[]{:T(128)}, f32[10,32]{1,0:T(8,128)S(1)}, bf16[10,512,512]{2,1,0:T(8,128)(2,1)}, bf16[2048,512]{0,1:T(8,128)(2,1)}, s32[]{:T(128)}, ...), condition=%wide.region_3.4_spmd, body=%wide.region_0.3_spmd.sunk | while | flops 1076887552 | bytes 4752341 | solution.py:52
  41.7 3.7 %fusion.12 = f32[2048]{0:T(1024)S(1)} fusion(bf16[2048,512]{0,1:T(8,128)(2,1)} %get-tuple-element.95, bf16[10,512,512]{2,1,0:T(8,128)(2,1)} %get-tuple-element.94, s32[]{:T(128)} %get-tuple-element.85), kind=kOutput, calls=%fused_computation.1.clone.1 | convolution fusion | flops 1076885504 | bytes 4727296 | tf_op jit(solution)/shard_map/while/body/eval_jaxpr/dot_general | solution.py:49
  45.7 3.7 %fusion.12 = f32[2048]{0:T(1024)S(1)} fusion(bf16[2048,512]{0,1:T(8,128)(2,1)} %get-tuple-element.95, bf16[10,512,512]{2,1,0:T(8,128)(2,1)} %get-tuple-element.94, s32[]{:T(128)} %get-tuple-element.85), kind=kOutput, calls=%fused_computation.1.clone.1 | convolution fusion | flops 1076885504 | bytes 4727296 | tf_op jit(solution)/shard_map/while/body/eval_jaxpr/dot_general | solution.py:49
  49.6 3.7 %fusion.12 = f32[2048]{0:T(1024)S(1)} fusion(bf16[2048,512]{0,1:T(8,128)(2,1)} %get-tuple-element.95, bf16[10,512,512]{2,1,0:T(8,128)(2,1)} %get-tuple-element.94, s32[]{:T(128)} %get-tuple-element.85), kind=kOutput, calls=%fused_computation.1.clone.1 | convolution fusion | flops 1076885504 | bytes 4727296 | tf_op jit(solution)/shard_map/while/body/eval_jaxpr/dot_general | solution.py:49
  53.5 3.7 %fusion.12 = f32[2048]{0:T(1024)S(1)} fusion(bf16[2048,512]{0,1:T(8,128)(2,1)} %get-tuple-element.95, bf16[10,512,512]{2,1,0:T(8,128)(2,1)} %get-tuple-element.94, s32[]{:T(128)} %get-tuple-element.85), kind=kOutput, calls=%fused_computation.1.clone.1 | convolution fusion | flops 1076885504 | bytes 4727296 | tf_op jit(solution)/shard_map/while/body/eval_jaxpr/dot_general | solution.py:49
  57.4 3.7 %fusion.12 = f32[2048]{0:T(1024)S(1)} fusion(bf16[2048,512]{0,1:T(8,128)(2,1)} %get-tuple-element.95, bf16[10,512,512]{2,1,0:T(8,128)(2,1)} %get-tuple-element.94, s32[]{:T(128)} %get-tuple-element.85), kind=kOutput, calls=%fused_computation.1.clone.1 | convolution fusion | flops 1076885504 | bytes 4727296 | tf_op jit(solution)/shard_map/while/body/eval_jaxpr/dot_general | solution.py:49
  61.4 3.7 %fusion.12 = f32[2048]{0:T(1024)S(1)} fusion(bf16[2048,512]{0,1:T(8,128)(2,1)} %get-tuple-element.95, bf16[10,512,512]{2,1,0:T(8,128)(2,1)} %get-tuple-element.94, s32[]{:T(128)} %get-tuple-element.85), kind=kOutput, calls=%fused_computation.1.clone.1 | convolution fusion | flops 1076885504 | bytes 4727296 | tf_op jit(solution)/shard_map/while/body/eval_jaxpr/dot_general | solution.py:49
  65.3 3.7 %fusion.12 = f32[2048]{0:T(1024)S(1)} fusion(bf16[2048,512]{0,1:T(8,128)(2,1)} %get-tuple-element.95, bf16[10,512,512]{2,1,0:T(8,128)(2,1)} %get-tuple-element.94, s32[]{:T(128)} %get-tuple-element.85), kind=kOutput, calls=%fused_computation.1.clone.1 | convolution fusion | flops 1076885504 | bytes 4727296 | tf_op jit(solution)/shard_map/while/body/eval_jaxpr/dot_general | solution.py:49
  69.2 3.7 %fusion.12 = f32[2048]{0:T(1024)S(1)} fusion(bf16[2048,512]{0,1:T(8,128)(2,1)} %get-tuple-element.95, bf16[10,512,512]{2,1,0:T(8,128)(2,1)} %get-tuple-element.94, s32[]{:T(128)} %get-tuple-element.85), kind=kOutput, calls=%fused_computation.1.clone.1 | convolution fusion | flops 1076885504 | bytes 4727296 | tf_op jit(solution)/shard_map/while/body/eval_jaxpr/dot_general | solution.py:49
  73.2 3.7 %fusion.12 = f32[2048]{0:T(1024)S(1)} fusion(bf16[2048,512]{0,1:T(8,128)(2,1)} %get-tuple-element.95, bf16[10,512,512]{2,1,0:T(8,128)(2,1)} %get-tuple-element.94, s32[]{:T(128)} %get-tuple-element.85), kind=kOutput, calls=%fused_computation.1.clone.1 | convolution fusion | flops 1076885504 | bytes 4727296 | tf_op jit(solution)/shard_map/while/body/eval_jaxpr/dot_general | solution.py:49
  77.1 3.7 %fusion.12 = f32[2048]{0:T(1024)S(1)} fusion(bf16[2048,512]{0,1:T(8,128)(2,1)} %get-tuple-element.95, bf16[10,512,512]{2,1,0:T(8,128)(2,1)} %get-tuple-element.94, s32[]{:T(128)} %get-tuple-element.85), kind=kOutput, calls=%fused_computation.1.clone.1 | convolution fusion | flops 1076885504 | bytes 4727296 | tf_op jit(solution)/shard_map/while/body/eval_jaxpr/dot_general | solution.py:49
  81.0 0.7 multiply_reduce_fusion
  81.9 11.0 %all-gather.3 = f32[4,1,40]{2,1,0:T(1,128)S(1)} all-gather(f32[1,1,40]{2,1,0:T(1,128)S(1)} %dynamic_update_slice.9), channel_id=1, replica_groups=mesh['ma_0'=4,'ma_1'=4,'ma_2'=2,'band'=4] {'ma_0'}, dimensions={0}, use_global_device_ids=true | all-gather | bytes 800 | tf_op jit(solution)/shard_map/all_gather | solution.py:29
  93.2 10.5 %all-reduce.8 = (f32[160]{0:T(256)S(1)}, f32[4]{0:T(128)S(1)}) all-reduce(f32[160]{0:T(256)S(1)} %dynamic-update-slice, f32[4]{0:T(128)S(1)} %dynamic-update-slice.4), channel_id=2, replica_groups=mesh['ma_0'=4,'ma_1'=4,'ma_2'=2,'band'=4] {'ma_1'}, use_global_device_ids=true, to_apply=%add | all-reduce | flops 164 | bytes 1312
  104.5 1.4 %dynamic-update-slice.5 = f32[2]{0:T(128)S(1)} dynamic-update-slice(f32[2]{0:T(128)S(1)} %broadcast.20, f32[1]{0:T(128)} %bitcast.13, u32[]{:T(128)} %bitcast.14) | dynamic-update-slice | bytes 12
  105.9 2.4 %all-reduce.9 = (f32[80]{0:T(128)S(1)}, f32[2]{0:T(128)S(1)}) all-reduce(f32[80]{0:T(128)S(1)} %dynamic-update-slice.1, f32[2]{0:T(128)S(1)} %dynamic-update-slice.5), channel_id=3, replica_groups=mesh['ma_0'=4,'ma_1'=4,'ma_2'=2,'band'=4] {'ma_2'}, use_global_device_ids=true, to_apply=%add.1 | all-reduce | flops 82 | bytes 656
  109.0 1.4 %dynamic-update-slice.6 = f32[4]{0:T(128)S(1)} dynamic-update-slice(f32[4]{0:T(128)S(1)} %broadcast.21, f32[1]{0:T(128)} %bitcast.15, u32[]{:T(128)} %bitcast.16) | dynamic-update-slice | bytes 12
  110.6 9.0 %all-reduce.7 = (f32[160]{0:T(256)S(1)}, f32[4]{0:T(128)S(1)}) all-reduce(f32[160]{0:T(256)S(1)} %dynamic-update-slice.2, f32[4]{0:T(128)S(1)} %dynamic-update-slice.6), channel_id=4, replica_groups=mesh['ma_0'=4,'ma_1'=4,'ma_2'=2,'band'=4] {'band'}, use_global_device_ids=true, to_apply=%add.2 | all-reduce | flops 164 | bytes 1312
  119.7 0.7 reduce_sum.115
  120.4 1.3 %multiply_divide_fusion = f32[10]{0:T(128)} fusion(f32[40]{0:T(128)S(1)} %reduce_sum.110, s32[]{:T(128)S(6)} %select_n.9, f32[]{:T(128)} %reduce_sum.115), kind=kLoop, calls=%fused_computation.12 | loop fusion | flops 20 | bytes 88 | tf_op jit(solution)/shard_map/div | solution.py:72
  (65 shorter events, 6.3 us)
Async XLA Ops:
  6.7 6.2 %copy-start = (s32[8]{0:T(128)S(1)}, s32[8]{0:T(128)}, u32[]{:S(2)}) copy-start(s32[8]{0:T(128)} %param.11) | copy-start | bytes 100
  6.7 7.5 %copy-start.4 = (u32[128]{0:T(128)S(1)}, u32[128]{0:T(128)}, u32[]{:S(2)}) copy-start(u32[128]{0:T(128)} %constant.56) | copy-start | bytes 1540
  6.7 20.6 %copy-start.3 = (u32[128]{0:T(128)S(1)}, u32[128]{0:T(128)}, u32[]{:S(2)}) copy-start(u32[128]{0:T(128)} %constant.41) | copy-start | bytes 1540
  6.7 21.2 %copy-start.2 = (u32[128]{0:T(128)S(1)}, u32[128]{0:T(128)}, u32[]{:S(2)}) copy-start(u32[128]{0:T(128)} %constant.46) | copy-start | bytes 1540
  6.7 23.0 %copy-start.1 = (u32[128]{0:T(128)S(1)}, u32[128]{0:T(128)}, u32[]{:S(2)}) copy-start(u32[128]{0:T(128)} %constant.51) | copy-start | bytes 1540
  8.4 30.9 %all-to-all-start = ((bf16[4,8,64,512]{3,2,1,0:T(8,128)(2,1)}), bf16[4,8,64,512]{3,2,1,0:T(8,128)(2,1)S(1)}, u32[]{:S(2)}, u32[]{:S(2)}) async-start(bf16[4,8,64,512]{3,2,1,0:T(8,128)(2,1)} %broadcast_in_dim.23), calls=%async_computation | async-start | bytes 4194304 | tf_op jit(solution)/shard_map/all_to_all | solution.py:13
